TPU v7x, 1024 devices: a whole 8x8x8 slice. The times are simulated.
1024 devices in a mesh: rows: 64 (over y, x), vecs: 16 (over z, core).
Axes of the slice: x: 8, y: 8, z: 8, core: 2. Of those that a mesh axis runs over, the one named last changes fastest.
Arguments:
- vectors: float32 [8192, 2048], P('rows', 'vecs'), may hold values from -6 to 6
- reflectors: float32 [3, 64, 128, 256], P(None, 'rows', 'vecs'), may hold values from -3 to 3
Outputs:
- transformed: float32 [8192, 2048], P('rows', 'vecs')
All inputs are finite; a program needn't handle non-finite values.
Results may differ from a plain program's by a relative error of at most 0.0003.
Values sent between devices are 32-bit elements; how exact they have to be, the bound alone decides.
A program may use at most 32 MiB of HBM per device.

v0:
```python
import jax
import jax.numpy as jnp
from jax import lax
from jax.sharding import PartitionSpec as P

HIGHEST = lax.Precision.HIGHEST


def from_behind(value, axis, steps):
    count = lax.axis_size(axis)
    leading, last = (max(0, -steps), min(count, count - steps))
    return lax.ppermute(value, axis, [(source, source + steps) for source in range(leading, last)])


def carried_in(part, axis, combine, identity):
    place = lax.axis_index(axis)
    gathered = jax.tree.map(lambda a: lax.all_gather(a, axis), part)
    state = jax.tree.map(lambda a, e: jnp.zeros_like(a) + jnp.asarray(e, a.dtype), part, identity)

    def one(hop, state):
        return combine(
            state, jax.tree.map(lambda a: lax.dynamic_index_in_dim(a, hop, 0, False), gathered)
        )

    return lax.fori_loop(0, place, one, state)


def inverse_factor(reflector):
    block_size = reflector.shape[0]
    gram_matrix = jnp.dot(reflector, reflector.T, precision=HIGHEST)
    half_diag = jnp.diag(gram_matrix) * 0.5
    nilpotent = jnp.triu(gram_matrix, 1) / half_diag[:, None]
    identity = jnp.eye(block_size, dtype=jnp.float32)
    power = -nilpotent
    result = identity + power
    reach = 2
    while reach < block_size:
        power = jnp.dot(power, power, precision=HIGHEST)
        result = jnp.dot(result, identity + power, precision=HIGHEST)
        reach = reach * 2
    return result / half_diag[None, :]


def reflect(window_rows, reflector, inv_matrix):
    weights = jnp.dot(reflector, window_rows, precision=HIGHEST)
    solved = jnp.dot(inv_matrix, weights, precision=HIGHEST)
    return window_rows - jnp.dot(reflector.T, solved, precision=HIGHEST)


def apply_blocks(slab_work, group_blocks, group_inverses):
    window_rows = slab_work
    updated = reflect(window_rows, group_blocks[0], group_inverses[0])
    slab_work = lax.dynamic_update_slice_in_dim(slab_work, updated, 0, 0)
    return slab_work


def compose(earlier, later):
    map_early, add_early = earlier
    map_late, add_late = later
    return (
        jnp.dot(map_late, map_early, precision=HIGHEST),
        jnp.dot(map_late, add_early, precision=HIGHEST) + add_late,
    )


def local(vectors, reflectors):
    rows_local, cols_local = vectors.shape
    block_size = reflectors.shape[3] // 2
    row_index = lax.axis_index("rows")
    row_count = lax.axis_size("rows")
    gathered = lax.all_gather(reflectors, "vecs", axis=2, tiled=True)
    row_pos = lax.broadcasted_iota(jnp.int32, gathered.shape, 3)
    block_pos = lax.broadcasted_iota(jnp.int32, gathered.shape, 1)
    cut_mask = (
        (row_index == row_count - 1)
        & (block_pos == gathered.shape[1] - 1)
        & (row_pos >= block_size)
    )
    gathered = jnp.where(cut_mask, jnp.zeros_like(gathered), gathered)
    inverses = jax.vmap(jax.vmap(inverse_factor))(gathered)
    identity = jnp.eye(block_size, dtype=jnp.float32)
    basis = jnp.concatenate([identity, jnp.zeros((rows_local, block_size), jnp.float32)], 0)
    is_first = row_index == 0
    current = vectors
    for group in range(gathered.shape[0]):
        top_rows = current
        below_rows = from_behind(top_rows, "rows", -1)
        slab_work = jnp.concatenate(
            [jnp.zeros((block_size, cols_local), jnp.float32), current[block_size:], below_rows], 0
        )
        joined = apply_blocks(
            jnp.concatenate([slab_work, basis], 1), gathered[group], inverses[group]
        )
        zero_carry = joined[:, :cols_local]
        carry_action = joined[:, cols_local:]
        step_map = carry_action[rows_local:]
        step_add = zero_carry[rows_local:]
        start_add = jnp.dot(step_map, top_rows, precision=HIGHEST) + step_add
        element = (
            jnp.where(is_first, jnp.zeros_like(step_map), step_map),
            jnp.where(is_first, start_add, step_add),
        )
        prefix_map = carried_in(
            element, "rows", compose, (identity, jnp.zeros((block_size, cols_local), jnp.float32))
        )
        carry_rows = jnp.where(is_first, top_rows, prefix_map[1])
        current = zero_carry[:rows_local] + jnp.dot(
            carry_action[:rows_local], carry_rows, precision=HIGHEST
        )
    return current


def solution(mesh):
    placed = (P("rows", "vecs"), P(None, "rows", "vecs", None))
    return jax.shard_map(
        local, mesh=mesh, in_specs=placed, out_specs=P("rows", "vecs"), check_vma=False
    )
```

profile of v0, /device:TPU:126, one launch (start us, length us, event | category | flops | bytes accessed | tf_op | source)
XLA Modules:
  0.0 827.0 jit_solution(18324386898706606228)
XLA Ops:
  6.5 3.3 collective-permute-start
  10.0 30.8 %all_gather.39 = f32[3,1,128,256]{3,2,1,0:T(8,128)S(1)} all-gather(f32[3,1,8,256]{3,2,1,0:T(8,128)} %param.9), channel_id=1, replica_groups=mesh['rows'=64,'vecs'=16] {'vecs'}, dimensions={2}, use_global_device_ids=true | all-gather | bytes 417792 | tf_op jit(solution)/shard_map/all_gather | solution.py:71
  41.3 4.7 copy.3
  46.0 1.7 gather_fusion
  54.7 83.1 %all-gather.13.cloned.1.call-done = f32[8192,128]{1,0:T(8,128)} async-done(((f32[128,128]{1,0:T(8,128)}), f32[8192,128]{1,0:T(8,128)}) %all-gather.13.cloned.1.call-update) | async-done | bytes 4194320 | tf_op jit(solution)/shard_map/all_gather | solution.py:17
  137.8 93.8 %all-gather.15.cloned.1.call-done = f32[8192,128]{1,0:T(8,128)} async-done(((f32[128,128]{1,0:T(8,128)}), f32[8192,128]{1,0:T(8,128)}) %all-gather.15.cloned.1.call-update) | async-done | bytes 4194320 | tf_op jit(solution)/shard_map/all_gather | solution.py:17
  231.7 71.0 %while.36 = (s32[]{:T(128)}, f32[128,128]{1,0:T(8,128)S(1)}, s32[]{:T(128)}, f32[64,128,128]{2,1,0:T(8,128)}, f32[64,128,128]{2,1,0:T(8,128)}, /*index=5*/s32[]{:T(128)}, s32[]{:T(128)}, s32[]{:T(128)}) while((s32[]{:T(128)}, f32[128,128]{1,0:T(8,128)S(1)}, s32[]{:T(128)}, f32[64,128,128]{2,1,0:T(8,128)}, f32[64,128,128]{2,1,0:T(8,128)}, ...), condition=%wide.region_1.2_spmd, body=%wide.region_0.1_spmd.sunk | while | flops 25182212 | bytes 394359 | solution.py:25
  302.9 1.8 collective-permute-start.1
  304.7 1.9 collective-permute-done.1
  309.2 87.1 %all-gather.19.cloned.1.call-done = f32[8192,128]{1,0:T(8,128)} async-done(((f32[128,128]{1,0:T(8,128)}), f32[8192,128]{1,0:T(8,128)}) %all-gather.19.cloned.1.call-update) | async-done | bytes 4194320 | tf_op jit(solution)/shard_map/all_gather | solution.py:17
  396.3 93.7 %all-gather.17.cloned.1.call-done = f32[8192,128]{1,0:T(8,128)} async-done(((f32[128,128]{1,0:T(8,128)}), f32[8192,128]{1,0:T(8,128)}) %all-gather.17.cloned.1.call-update) | async-done | bytes 4194320 | tf_op jit(solution)/shard_map/all_gather | solution.py:17
  490.0 71.1 %while.37 = (s32[]{:T(128)}, f32[128,128]{1,0:T(8,128)S(1)}, s32[]{:T(128)}, f32[64,128,128]{2,1,0:T(8,128)}, f32[64,128,128]{2,1,0:T(8,128)}, /*index=5*/s32[]{:T(128)}, s32[]{:T(128)}, s32[]{:T(128)}) while((s32[]{:T(128)}, f32[128,128]{1,0:T(8,128)S(1)}, s32[]{:T(128)}, f32[64,128,128]{2,1,0:T(8,128)}, f32[64,128,128]{2,1,0:T(8,128)}, ...), condition=%wide.region_3.4_spmd, body=%wide.region_2.3_spmd.sunk | while | flops 25182212 | bytes 394359 | solution.py:25
  503.5 1.1 convolution_add_fusion.11
  505.8 1.1 convolution_add_fusion.11
  508.0 1.1 convolution_add_fusion.11
  510.3 1.1 convolution_add_fusion.11
  512.5 1.1 convolution_add_fusion.11
  523.8 1.1 convolution_add_fusion.11
  526.1 1.1 convolution_add_fusion.11
  528.3 1.1 convolution_add_fusion.11
  530.6 1.1 convolution_add_fusion.11
  532.8 1.1 convolution_add_fusion.11
  535.1 1.1 convolution_add_fusion.11
  546.4 1.1 convolution_add_fusion.11
  548.6 1.1 convolution_add_fusion.11
  550.9 1.1 convolution_add_fusion.11
  553.2 1.1 convolution_add_fusion.11
  561.2 1.9 collective-permute-start.2
  563.1 1.9 collective-permute-done.2
  567.5 87.1 %all-gather.23.cloned.1.call-done = f32[8192,128]{1,0:T(8,128)} async-done(((f32[128,128]{1,0:T(8,128)}), f32[8192,128]{1,0:T(8,128)}) %all-gather.23.cloned.1.call-update) | async-done | bytes 4194320 | tf_op jit(solution)/shard_map/all_gather | solution.py:17
  654.6 93.7 %all-gather.21.cloned.1.call-done = f32[8192,128]{1,0:T(8,128)} async-done(((f32[128,128]{1,0:T(8,128)}), f32[8192,128]{1,0:T(8,128)}) %all-gather.21.cloned.1.call-update) | async-done | bytes 4194320 | tf_op jit(solution)/shard_map/all_gather | solution.py:17
  748.4 71.0 %while.38 = (s32[]{:T(128)}, f32[128,128]{1,0:T(8,128)S(1)}, s32[]{:T(128)}, f32[64,128,128]{2,1,0:T(8,128)}, f32[64,128,128]{2,1,0:T(8,128)}, /*index=5*/s32[]{:T(128)}, s32[]{:T(128)}, s32[]{:T(128)}) while((s32[]{:T(128)}, f32[128,128]{1,0:T(8,128)S(1)}, s32[]{:T(128)}, f32[64,128,128]{2,1,0:T(8,128)}, f32[64,128,128]{2,1,0:T(8,128)}, ...), condition=%wide.region_5.6_spmd, body=%wide.region_4.5_spmd.sunk | while | flops 25182212 | bytes 394359 | solution.py:25
  (419 shorter events, 202.9 us)
Async XLA Ops:
  6.5 131.3 %all-gather.13.cloned.1.call-start = ((), (), s32[]{:S(2)}) async-start(), calls=%async_computation | async-start | bytes 4259840 | tf_op jit(solution)/shard_map/all_gather | solution.py:17
  6.5 45.5 %collective-permute-start = (f32[128,128]{1,0:T(8,128)}, f32[128,128]{1,0:T(8,128)S(1)}, u32[]{:S(2)}, u32[]{:S(2)}) collective-permute-start(f32[128,128]{1,0:T(8,128)} %param.8), channel_id=1, source_target_pairs={{16,0},{32,16},{48,32},{64,48},{80,64},{96,80},{112,96},{128,112},... | collective-permute-start | bytes 196616 | tf_op jit(solution)/shard_map/ppermute | solution.py:12
  48.6 5.1 copy-start
  53.7 177.9 %all-gather.15.cloned.1.call-start = ((), (), s32[]{:S(2)}) async-start(), calls=%async_computation.1 | async-start | bytes 4259840 | tf_op jit(solution)/shard_map/all_gather | solution.py:17
  54.6 341.6 %all-gather.19.cloned.1.call-start = ((), (), s32[]{:S(2)}) async-start(), calls=%async_computation.3 | async-start | bytes 4259840 | tf_op jit(solution)/shard_map/all_gather | solution.py:17
  302.9 3.7 collective-permute-start.1
  308.4 181.5 %all-gather.17.cloned.1.call-start = ((), (), s32[]{:S(2)}) async-start(), calls=%async_computation.2 | async-start | bytes 4259840 | tf_op jit(solution)/shard_map/all_gather | solution.py:17
  309.2 345.5 %all-gather.23.cloned.1.call-start = ((), (), s32[]{:S(2)}) async-start(), calls=%async_computation.5 | async-start | bytes 4259840 | tf_op jit(solution)/shard_map/all_gather | solution.py:17
  561.2 3.7 collective-permute-start.2
  566.8 181.5 %all-gather.21.cloned.1.call-start = ((), (), s32[]{:S(2)}) async-start(), calls=%async_computation.4 | async-start | bytes 4259840 | tf_op jit(solution)/shard_map/all_gather | solution.py:17
Sparse Core Ops, SparseCore 0:
  53.8 83.9 all-gather.12
  142.0 89.5 all-gather.14
  308.6 87.6 all-gather.18
  400.3 89.5 all-gather.16
  567.0 87.6 all-gather.22
  658.7 89.5 all-gather.20
where the time goes:
time: 836 us; the launch traced here: 827 us
  waiting for transfers between devices  542 us (65%)
  matrix products  216 us (26%)
  blocking collectives  30.8 us (4%)
  between operations  13.8 us (2%)
    all_gather x6, waiting for transfers between devices, carried_in(): gathered = jax.tree.map(lambda a: lax.all_gather(a, axis), part)  539 us
    dot_general x189, matrix products, compose(): jnp.dot(map_late, add_early, precision=HIGHEST) + add_late  204 us
    all_gather x1, blocking collectives, local(): gathered = lax.all_gather(reflectors, 'vecs', axis=2, tiled=True)  30.8 us
  transfers between devices with their start and end apart: 9, of which 8 were waited for; matrix products, arithmetic and copies ran while one was open for 2% of the time, Pallas kernels for 0%

commit v1 on v0

v1 whole, which is shorter than its diff:
```python
import functools

import jax
import jax.numpy as jnp
from jax import lax
from jax.experimental import pallas as pl
from jax.experimental.pallas import tpu as pltpu
from jax.sharding import PartitionSpec as P

HIGHEST = lax.Precision.HIGHEST
MESH = pl.DeviceIdType.MESH
CHUNK = 32


def hdot(a, b):
    return jnp.dot(a, b, precision=HIGHEST, preferred_element_type=jnp.float32)


def split(value):
    high = value.astype(jnp.bfloat16)
    low = (value - high.astype(jnp.float32)).astype(jnp.bfloat16)
    return high, low


def unit_lower_inverse(strict):
    n = strict.shape[0]
    row = lax.broadcasted_iota(jnp.int32, (n, n), 0)
    col = lax.broadcasted_iota(jnp.int32, (n, n), 1)
    result = jnp.where(row == col, 1.0, 0.0).astype(jnp.float32)
    size = 1
    while size < n:
        wide = 2 * size
        pair = (row // wide == col // wide) & (row % wide >= size) & (col % wide < size)
        corner = jnp.where(pair, strict, 0.0)
        if size == 1:
            result = result - corner
        else:
            result = result - hdot(hdot(result, corner), result)
        size = wide
    return result


def block_map(block):
    n = block.shape[0]
    gram = lax.dot_general(block, block, (((1,), (1,)), ((), ())), precision=HIGHEST, preferred_element_type=jnp.float32)
    row = lax.broadcasted_iota(jnp.int32, (n, n), 0)
    col = lax.broadcasted_iota(jnp.int32, (n, n), 1)
    diagonal = jnp.where(row == col, gram * 0.5, 0.0)
    half_row = jnp.sum(diagonal, axis=0, keepdims=True)
    half_col = jnp.sum(diagonal, axis=1, keepdims=True)
    strict = jnp.where(row > col, gram / half_row, 0.0)
    solved = hdot(unit_lower_inverse(strict), block) / half_col
    return hdot(block.T, solved)


def kernel(n_rows, n_vecs, x_ref, refl_ref, out_ref, blocks, maps, lower, carry, done, passed,
           ag_send, ag_recv, low_send, low_recv, car_send, car_recv):
    groups, size = blocks.shape[0], blocks.shape[1]
    cols = x_ref.shape[1]
    n_chunks = cols // CHUNK
    r, v = lax.axis_index("rows"), lax.axis_index("vecs")
    above, below = lax.rem(r + n_rows - 1, n_rows), lax.rem(r + 1, n_rows)
    first, last = r == 0, r == n_rows - 1
    piece = size // n_vecs
    n_chips = n_vecs // 2
    core = lax.rem(v, 2)
    partner = v + 1 - 2 * core
    others = [lax.rem(v + 2 * step, n_vecs) for step in range(1, n_chips)]
    sources = [lax.rem(v - 2 * step + n_vecs, n_vecs) for step in range(1, n_chips)]

    barrier = pltpu.get_barrier_semaphore()
    for peer in [(r, partner)] + [(r, other) for other in others] + [(above, v), (below, v)]:
        pl.semaphore_signal(barrier, inc=1, device_id=peer, device_id_type=MESH)
    pl.semaphore_wait(barrier, n_chips + 2)

    def rows_of(vec):
        return pl.ds(pl.multiple_of(vec * piece, piece), piece)

    sends = []
    for k, peer in enumerate(others + [partner]):
        sends.append(pltpu.make_async_remote_copy(
            refl_ref.at[:, 0], blocks.at[:, rows_of(v)], ag_send.at[k], ag_recv.at[v],
            device_id=(r, peer), device_id_type=MESH))
        sends[-1].start()

    done[0] = x_ref[...].T

    def lower_copy(g, j):
        at = pl.ds(j * CHUNK, CHUNK)
        return pltpu.make_async_remote_copy(
            done.at[g, at], lower.at[g, at], low_send.at[g, j], low_recv.at[g, j],
            device_id=(above, v), device_id_type=MESH)

    def carry_copy(g, j):
        at = pl.ds(j * CHUNK, CHUNK)
        return pltpu.make_async_remote_copy(
            passed.at[g, at], carry.at[g, at], car_send.at[g, j], car_recv.at[g, j],
            device_id=(below, v), device_id_type=MESH)

    @pl.when(jnp.logical_not(first))
    def _():
        for j in range(n_chunks):
            lower_copy(0, j).start()

    @pl.when(first)
    def _():
        carry[0] = done[0]

    @pl.when(last)
    def _():
        lower[...] = jnp.zeros_like(lower)

    blocks[:, rows_of(v)] = refl_ref[:, 0]

    def arrived(vec):
        pltpu.make_async_remote_copy(
            refl_ref.at[:, 0], blocks.at[:, rows_of(vec)], ag_send.at[0], ag_recv.at[vec],
            device_id=(r, partner), device_id_type=MESH).wait_recv()

    order = sorted(range(1, n_chips), key=lambda step: min(step, n_chips - step))
    for step in order:
        source = sources[step - 1]
        arrived(source)
        sends.append(pltpu.make_async_remote_copy(
            blocks.at[:, rows_of(source)], blocks.at[:, rows_of(source)],
            ag_send.at[n_chips + step - 1], ag_recv.at[source],
            device_id=(r, partner), device_id_type=MESH))
        sends[-1].start()
    arrived(partner)
    for step in order:
        arrived(lax.rem(partner - 2 * step + n_vecs, n_vecs))
    for copy in sends:
        copy.wait_send()

    wide = 2 * size
    keep = jnp.logical_not(last) | (lax.broadcasted_iota(jnp.int32, (size, wide), 1) < size)
    for g in range(groups):
        full = block_map(jnp.where(keep, blocks[g], 0.0))
        high, low = split(full)
        for part in range(2):
            at = slice(part * size, (part + 1) * size)
            maps[g, part, 0:size] = high[at]
            maps[g, part, size:2 * size] = high[at]
            maps[g, part, 2 * size:3 * size] = low[at]

    def product(value, g, part):
        high, low = split(value)
        return jnp.dot(jnp.concatenate([high, low, high], axis=1), maps[g, part],
                       preferred_element_type=jnp.float32)

    for g in range(groups):
        for j in range(n_chunks):
            at = slice(j * CHUNK, (j + 1) * CHUNK)

            @pl.when(jnp.logical_not(last))
            def _():
                lower_copy(g, j).wait_recv()

            under = lower[g, at]
            base = product(under, g, 1)

            @pl.when(jnp.logical_not(first))
            def _():
                carry_copy(g, j).wait_recv()

            top = carry[g, at]
            taken = base + product(top, g, 0)
            passed[g, at] = under - taken[:, size:]

            @pl.when(jnp.logical_not(last))
            def _():
                carry_copy(g, j).start()

            final = top - taken[:, :size]
            if g == groups - 1:
                out_ref[at] = final
            else:
                done[g + 1, at] = final

                @pl.when(jnp.logical_not(first))
                def _():
                    lower_copy(g + 1, j).start()

                @pl.when(first)
                def _():
                    carry[g + 1, at] = final

    @pl.when(jnp.logical_not(last))
    def _():
        for g in range(groups):
            for j in range(n_chunks):
                carry_copy(g, j).wait_send()

    @pl.when(jnp.logical_not(first))
    def _():
        for g in range(groups):
            for j in range(n_chunks):
                lower_copy(g, j).wait_send()


def local(n_rows, n_vecs, vectors, reflectors):
    size, cols = vectors.shape
    groups, wide = reflectors.shape[0], reflectors.shape[3]
    n_chunks = cols // CHUNK
    slab = pltpu.VMEM((groups, cols, size), jnp.float32)
    dma = pltpu.SemaphoreType.DMA
    out = pl.pallas_call(
        functools.partial(kernel, n_rows, n_vecs),
        out_shape=jax.ShapeDtypeStruct((cols, size), jnp.float32),
        in_specs=[pl.BlockSpec(memory_space=pltpu.VMEM)] * 2,
        out_specs=pl.BlockSpec(memory_space=pltpu.VMEM),
        scratch_shapes=[
            pltpu.VMEM((groups, size, wide), jnp.float32),
            pltpu.VMEM((groups, 2, 3 * size, wide), jnp.bfloat16),
            slab, slab, slab, slab,
            dma((n_vecs,)), dma((n_vecs,)),
            dma((groups, n_chunks)), dma((groups, n_chunks)),
            dma((groups, n_chunks)), dma((groups, n_chunks)),
        ],
        compiler_params=pltpu.CompilerParams(collective_id=0, has_side_effects=True),
        name="chain",
    )(vectors, reflectors)
    return out.T


def solution(mesh):
    n_rows, n_vecs = mesh.shape["rows"], mesh.shape["vecs"]
    placed = (P("rows", "vecs"), P(None, "rows", "vecs", None))
    return jax.shard_map(
        functools.partial(local, n_rows, n_vecs), mesh=mesh, in_specs=placed,
        out_specs=P("rows", "vecs"), check_vma=False)
```

time: 836 us -> 256 us (0.31); the launches traced: 827 us -> 256 us
  waiting for transfers between devices: 542 us -> 0 us
  Pallas kernels: 0 us -> 254 us
  matrix products: 216 us -> 0 us
  blocking collectives: 30.8 us -> 0 us
  between operations: 13.8 us -> 0.01 us
    all_gather x6 -> x0, waiting for transfers between devices: 539 us -> none  [carried_in(): gathered = jax.tree.map(lambda a: lax.all_gather(a, axis), part)]
    pallas_call x0 -> x1, Pallas kernels: none -> 254 us  [local(): pl.pallas_call(functools.partial(kernel, n_rows, n_vecs), out_shape=jax.S...]
    dot_general x217 -> x0, matrix products: 216 us -> none  [the longest x189 204 us: compose(): jnp.dot(map_late, add_early, precision=HIGHEST) + add_late]
    all_gather x1 -> x0, blocking collectives: 30.8 us -> none  [local(): gathered = lax.all_gather(reflectors, 'vecs', axis=2, tiled=True)]
  transfers between devices with their start and end apart: 9 -> 0, of which waited for: 8 -> 0; matrix products, arithmetic and copies ran while one was open for 2% -> 0% of each run, Pallas kernels for 0% -> 0%
where the time goes in v1:
time: 256 us
  Pallas kernels  254 us (99%)
    pallas_call x1, Pallas kernels, local(): pl.pallas_call(functools.partial(kernel, n_rows, n_vecs), out_shape=jax.S...  254 us

profile of v1, /device:TPU:126, one launch (start us, length us, event | category | flops | bytes accessed | tf_op | source)
XLA Modules:
  0.0 255.7 jit_solution(7380243218377703861)
XLA Ops:
  0.0 254.2 %chain.1 = f32[128,128]{1,0:T(8,128)} custom-call(f32[128,128]{1,0:T(8,128)} %x_ref.1, f32[3,1,8,256]{3,2,1,0:T(8,128)} %refl_ref.1), custom_call_target="tpu_custom_call" | custom-call | tf_op jit(solution)/shard_map/chain/pallas_call | solution.py:207
  254.2 1.6 copy.3

commit v2 on v1

v2 whole, which is shorter than its diff:
```python
import functools

import jax
import jax.numpy as jnp
from jax import lax
from jax.experimental import pallas as pl
from jax.experimental.pallas import tpu as pltpu
from jax.sharding import PartitionSpec as P

HIGHEST = lax.Precision.HIGHEST
MESH = pl.DeviceIdType.MESH
ACROSS = 8


def hdot(a, b):
    return jnp.dot(a, b, precision=HIGHEST, preferred_element_type=jnp.float32)


def split(value):
    high = value.astype(jnp.bfloat16)
    low = (value - high.astype(jnp.float32)).astype(jnp.bfloat16)
    return high, low


def inverse_factors(blocks):
    n = blocks[0].shape[0]
    row = lax.broadcasted_iota(jnp.int32, (n, n), 0)
    col = lax.broadcasted_iota(jnp.int32, (n, n), 1)
    stricts, halves = [], []
    for block in blocks:
        gram = lax.dot_general(block, block, (((1,), (1,)), ((), ())), precision=HIGHEST,
                               preferred_element_type=jnp.float32)
        diagonal = jnp.where(row == col, gram * 0.5, 0.0)
        halves.append(jnp.sum(diagonal, axis=1, keepdims=True))
        stricts.append(jnp.where(row > col, gram / jnp.sum(diagonal, axis=0, keepdims=True), 0.0))
    identity = jnp.where(row == col, 1.0, 0.0).astype(jnp.float32)
    results = [identity] * len(blocks)
    size = 1
    while size < n:
        wide = 2 * size
        pair = (row // wide == col // wide) & (row % wide >= size) & (col % wide < size)
        corners = [jnp.where(pair, strict, 0.0) for strict in stricts]
        if size == 1:
            results = [result - corner for result, corner in zip(results, corners)]
        else:
            halfway = [hdot(result, corner) for result, corner in zip(results, corners)]
            results = [result - hdot(half, result) for result, half in zip(results, halfway)]
        size = wide
    return [result / half for result, half in zip(results, halves)]


def kernel(n_rows, n_vecs, nx, x_ref, refl_ref, out_ref, blocks, factors, maps, turned, state, base, carry,
           passed, ready, final, ag_send, ag_recv, in_send, in_recv, ring_send, ring_recv, share_send,
           share_recv, low_send, low_recv, car_send, car_recv, fin_send, fin_recv):
    groups, size, wide = blocks.shape[1:]
    cols = x_ref.shape[1]
    part = cols // nx
    ny = n_rows // nx
    n_chips = n_vecs // 2
    piece = size // n_vecs
    r, v = lax.axis_index("rows"), lax.axis_index("vecs")
    y, x = r // nx, lax.rem(r, nx)
    core = lax.rem(v, 2)
    partner = v + 1 - 2 * core
    first, last = y == 0, y == ny - 1
    inner, outer = jnp.logical_not(first), jnp.logical_not(last)
    above = (lax.rem(r + n_rows - nx, n_rows), v)
    below = (lax.rem(r + nx, n_rows), v)
    mate = (r, partner)
    way = 1 - 2 * core

    def along(step):
        return lax.rem(x + step + 2 * nx, nx)

    def remote(src, dst, sent, got, device):
        return pltpu.make_async_remote_copy(src, dst, sent, got, device_id=device, device_id_type=MESH)

    onward = (y * nx + along(way), v)
    chips = [lax.rem(v + 2 * k, n_vecs) for k in range(1, n_chips)]
    peers = [along(k) for k in range(1, nx)]

    barrier = pltpu.get_barrier_semaphore()
    for device in [mate, above, below] + [(r, c) for c in chips] + [(y * nx + p, v) for p in peers]:
        pl.semaphore_signal(barrier, inc=1, device_id=device, device_id_type=MESH)
    pl.semaphore_wait(barrier, 3 + len(chips) + len(peers))

    def rows_of(vec):
        return pl.ds(pl.multiple_of(vec * piece, piece), piece)

    def cols_of(place):
        return pl.ds(pl.multiple_of(place * part, part), part)

    sends = []
    for k, peer in enumerate(chips + [partner]):
        sends.append(remote(refl_ref.at[:, 0], blocks.at[x, :, rows_of(v)], ag_send.at[k], ag_recv.at[v], (r, peer)))
        sends[-1].start()

    turned[...] = x_ref[...].T
    for k, peer in enumerate(peers):
        sends.append(remote(turned.at[cols_of(peer)], state.at[0, x], in_send.at[k], in_recv.at[x], (y * nx + peer, v)))
        sends[-1].start()
    state[0, x] = turned[cols_of(x)]
    blocks[x, :, rows_of(v)] = refl_ref[:, 0]

    @pl.when(last)
    def _():
        for g in range(groups):
            state[g, nx] = jnp.zeros((part, size), jnp.float32)

    def arrived(vec):
        remote(refl_ref.at[:, 0], blocks.at[x, :, rows_of(vec)], ag_send.at[0], ag_recv.at[vec], mate).wait_recv()

    order = sorted(range(1, n_chips), key=lambda k: min(k, n_chips - k))
    for k in order:
        source = lax.rem(v - 2 * k + n_vecs, n_vecs)
        arrived(source)
        there = blocks.at[x, :, rows_of(source)]
        sends.append(remote(there, there, ag_send.at[n_chips + k - 1], ag_recv.at[source], mate))
        sends[-1].start()
    arrived(partner)
    for k in order:
        arrived(lax.rem(partner - 2 * k + n_vecs, n_vecs))

    far = nx // 2
    stores = (blocks, factors)

    def ring(step, g, kind):
        there = stores[kind].at[along(-way * (step - 1)), g]
        return remote(there, there, ring_send.at[step - 1, g, kind], ring_recv.at[step - 1, g, kind], onward)

    def ring_arrival(step, g, kind):
        there = stores[kind].at[along(-way * step), g]
        return remote(there, there, ring_send.at[step - 1, g, kind], ring_recv.at[step - 1, g, kind], onward)

    def share(step, g, kind, sign):
        there = stores[kind].at[along(-sign * way * step), g]
        return remote(there, there, share_send.at[step - 1, g, kind], share_recv.at[step - 1, g, kind], mate)

    def owner(step, g, kind):
        if step < far:
            return None
        return 0 if g == 0 or (g == 1 and kind == 0) else 1

    def on(core_index, action):
        if core_index is None:
            action()
        else:
            pl.when(core == core_index)(action)

    for g in range(groups):
        on(owner(1, g, 0), lambda: ring(1, g, 0).start())

    for k in range(1, nx):
        source = along(-k)
        remote(turned.at[cols_of(x)], state.at[0, source], in_send.at[0], in_recv.at[source], onward).wait_recv()

    def low(g):
        return remote(state.at[g, 0], state.at[g, nx], low_send.at[g], low_recv.at[g], above)

    @pl.when(inner)
    def _():
        low(0).start()

    lane = lax.broadcasted_iota(jnp.int32, (size, wide), 1)

    def masked(place, g):
        return jnp.where((y * nx + place < n_rows - 1) | (lane < size), blocks[place, g], 0.0)

    for g, inverse in enumerate(inverse_factors([masked(x, g) for g in range(groups)])):
        factors[x, g] = inverse
        on(owner(1, g, 1), lambda: ring(1, g, 1).start())

    def form(place):
        def one(g, nothing):
            block = masked(place, g)
            full = hdot(block.T, hdot(factors[place, g], block))
            maps[place, g, 0], maps[place, g, 1] = split(full)
            return nothing

        lax.fori_loop(0, groups, one, 0)

    form(x)
    for step in range(1, far + 1):
        for kind in range(2):
            for g in range(groups):
                def take():
                    ring_arrival(step, g, kind).wait_recv()
                    if step < far:
                        on(owner(step + 1, g, kind), lambda: ring(step + 1, g, kind).start())
                    share(step, g, kind, 1).start()

                on(owner(step, g, kind), take)
        if step < far:
            form(along(-way * step))
        for kind in range(2):
            for g in range(groups):
                whose = owner(step, g, kind)
                on(None if whose is None else 1 - whose, lambda: share(step, g, kind, -1).wait_recv())
        form(along(way * step))

    def product(value, place, g, half):
        at = slice(half * size, (half + 1) * size)
        high, lower = split(value)
        both = jnp.dot(jnp.concatenate([high, lower], axis=0), maps[place, g, 0, at], preferred_element_type=jnp.float32)
        cross = jnp.dot(high, maps[place, g, 1, at], preferred_element_type=jnp.float32)
        return both[:part] + (both[part:] + cross)

    def pass_on(g):
        return remote(passed.at[g], carry.at[g], car_send.at[g], car_recv.at[g], below)

    def deliver(place, slot):
        return remote(ready.at[slot], final.at[cols_of(x)], fin_send.at[slot], fin_recv.at[x], (y * nx + place, v))

    def prepare(g, place):
        under = state[g, place + 1]
        taken = product(under, place, g, 1)
        base[place, :, :size] = -taken[:, :size]
        base[place, :, size:] = under - taken[:, size:]

    for g in range(groups):
        for place in range(nx - 1):
            prepare(g, place)

        @pl.when(first)
        def _():
            carry[g] = state[g, 0]

        @pl.when(inner)
        def _():
            pass_carry = pass_on(g)
            pass_carry.wait_recv()

        top = carry[g]
        for place in range(nx):
            if place == nx - 1:
                @pl.when(outer)
                def _():
                    low(g).wait_recv()

                prepare(g, place)
            result = base[place] - product(top, place, g, 0)
            done = top + result[:, :size]
            top = result[:, size:]
            if g < groups - 1:
                state[g + 1, place] = done
                if place == 0:
                    @pl.when(inner)
                    def _():
                        low(g + 1).start()
            else:
                ready[place] = done

                @pl.when(x != place)
                def _():
                    deliver(place, place).start()
        passed[g] = top

        @pl.when(outer)
        def _():
            pass_on(g).start()

    final[cols_of(x)] = ready[x]
    for k in range(1, nx):
        source = along(-k)
        remote(ready.at[0], final.at[cols_of(source)], fin_send.at[0], fin_recv.at[source], onward).wait_recv()
    out_ref[...] = final[...]

    for copy in sends:
        copy.wait_send()
    for step in range(1, far + 1):
        for kind in range(2):
            for g in range(groups):
                def finish():
                    ring(step, g, kind).wait_send()
                    share(step, g, kind, 1).wait_send()

                on(owner(step, g, kind), finish)
    for place in range(nx):
        @pl.when(x != place)
        def _():
            deliver(place, place).wait_send()

    @pl.when(outer)
    def _():
        for g in range(groups):
            pass_on(g).wait_send()

    @pl.when(inner)
    def _():
        for g in range(groups):
            low(g).wait_send()


def local(n_rows, n_vecs, nx, vectors, reflectors):
    size, cols = vectors.shape
    groups, wide = reflectors.shape[0], reflectors.shape[3]
    part, far, f32, vmem = cols // nx, nx // 2, jnp.float32, pltpu.VMEM
    dma = pltpu.SemaphoreType.DMA
    out = pl.pallas_call(
        functools.partial(kernel, n_rows, n_vecs, nx),
        out_shape=jax.ShapeDtypeStruct((cols, size), f32),
        in_specs=[pl.BlockSpec(memory_space=vmem)] * 2,
        out_specs=pl.BlockSpec(memory_space=vmem),
        scratch_shapes=[
            vmem((nx, groups, size, wide), f32),
            vmem((nx, groups, size, size), f32),
            vmem((nx, groups, 2, wide, wide), jnp.bfloat16),
            vmem((cols, size), f32),
            vmem((groups, nx + 1, part, size), f32),
            vmem((nx, part, wide), f32),
            vmem((groups, part, size), f32),
            vmem((groups, part, size), f32),
            vmem((nx, part, size), f32),
            vmem((cols, size), f32),
            dma((n_vecs,)), dma((n_vecs,)), dma((nx,)), dma((nx,)),
            dma((far, groups, 2)), dma((far, groups, 2)), dma((far, groups, 2)), dma((far, groups, 2)),
            dma((groups,)), dma((groups,)), dma((groups,)), dma((groups,)), dma((nx,)), dma((nx,)),
        ],
        compiler_params=pltpu.CompilerParams(collective_id=0, has_side_effects=True),
        name="rows",
    )(vectors, reflectors)
    return out.T


def solution(mesh):
    n_rows, n_vecs = mesh.shape["rows"], mesh.shape["vecs"]
    placed = (P("rows", "vecs"), P(None, "rows", "vecs", None))
    return jax.shard_map(
        functools.partial(local, n_rows, n_vecs, ACROSS), mesh=mesh, in_specs=placed,
        out_specs=P("rows", "vecs"), check_vma=False)
```

time: 256 us -> 105 us (0.41)
  Pallas kernels: 254 us -> 103 us
    pallas_call x1, Pallas kernels: 254 us -> 103 us  [local(): pl.pallas_call(functools.partial(kernel, n_rows, n_vecs, nx), out_shape=j...]
where the time goes in v2:
time: 105 us
  Pallas kernels  103 us (98%)
  local copies, waits for them, and re-layouts  1.57 us (1%)
    pallas_call x1, Pallas kernels, local(): pl.pallas_call(functools.partial(kernel, n_rows, n_vecs, nx), out_shape=j...  103 us

profile of v2, /device:TPU:126, one launch (start us, length us, event | category | flops | bytes accessed | tf_op | source)
XLA Modules:
  0.0 105.0 jit_solution(18376408752705869625)
XLA Ops:
  0.0 103.4 %rows.1 = f32[128,128]{1,0:T(8,128)} custom-call(f32[128,128]{1,0:T(8,128)} %x_ref.1, f32[3,1,8,256]{3,2,1,0:T(8,128)} %refl_ref.1), custom_call_target="tpu_custom_call" | custom-call | tf_op jit(solution)/shard_map/rows/pallas_call | solution.py:299
  103.4 1.6 %copy.3 = f32[128,128]{1,0:T(8,128)} copy(f32[128,128]{0,1:T(8,128)} %bitcast.1) | data formatting | bytes 131072 | tf_op jit(solution)/shard_map/transpose | solution.py:322

commit v3 on v2

--- a/solution.py
+++ b/solution.py
@@ -20,6 +20,15 @@
     high = value.astype(jnp.bfloat16)
     low = (value - high.astype(jnp.float32)).astype(jnp.bfloat16)
     return high, low
+
+
+def product3(left, right):
+    (left_high, left_low), (right_high, right_low) = split(left), split(right)
+
+    def dot(a, b):
+        return jnp.dot(a, b, preferred_element_type=jnp.float32)
+
+    return dot(left_high, right_high) + (dot(left_low, right_high) + dot(left_high, right_low))
 
 
 def inverse_factors(blocks):
@@ -49,7 +58,7 @@
     return [result / half for result, half in zip(results, halves)]
 
 
-def kernel(n_rows, n_vecs, nx, x_ref, refl_ref, out_ref, blocks, factors, maps, turned, state, base, carry,
+def kernel(n_rows, n_vecs, nx, x_ref, refl_ref, out_ref, blocks, factors, maps, turned, state, base, skip, carry,
            passed, ready, final, ag_send, ag_recv, in_send, in_recv, ring_send, ring_recv, share_send,
            share_recv, low_send, low_recv, car_send, car_recv, fin_send, fin_recv):
     groups, size, wide = blocks.shape[1:]
@@ -136,10 +145,8 @@
         there = stores[kind].at[along(-sign * way * step), g]
         return remote(there, there, share_send.at[step - 1, g, kind], share_recv.at[step - 1, g, kind], mate)
 
-    def owner(step, g, kind):
-        if step < far:
-            return None
-        return 0 if g == 0 or (g == 1 and kind == 0) else 1
+    def owner(step, kind):
+        return None if step < far else kind
 
     def on(core_index, action):
         if core_index is None:
@@ -147,8 +154,10 @@
         else:
             pl.when(core == core_index)(action)
 
-    for g in range(groups):
-        on(owner(1, g, 0), lambda: ring(1, g, 0).start())
+    def launch(g, kind):
+        on(owner(1, kind), lambda: ring(1, g, kind).start())
+
+    launch(0, 0)
 
     for k in range(1, nx):
         source = along(-k)
@@ -168,35 +177,34 @@
 
     for g, inverse in enumerate(inverse_factors([masked(x, g) for g in range(groups)])):
         factors[x, g] = inverse
-        on(owner(1, g, 1), lambda: ring(1, g, 1).start())
-
-    def form(place):
-        def one(g, nothing):
-            block = masked(place, g)
-            full = hdot(block.T, hdot(factors[place, g], block))
-            maps[place, g, 0], maps[place, g, 1] = split(full)
-            return nothing
-
-        lax.fori_loop(0, groups, one, 0)
-
-    form(x)
-    for step in range(1, far + 1):
-        for kind in range(2):
-            for g in range(groups):
+        if g == 0:
+            launch(0, 1)
+
+    def form(place, g):
+        block = masked(place, g)
+        full = product3(block.T, product3(factors[place, g], block))
+        maps[place, g, 0], maps[place, g, 1] = split(full)
+
+    def spread(g):
+        form(x, g)
+        for step in range(1, far + 1):
+            for kind in range(2):
                 def take():
                     ring_arrival(step, g, kind).wait_recv()
                     if step < far:
-                        on(owner(step + 1, g, kind), lambda: ring(step + 1, g, kind).start())
+                        on(owner(step + 1, kind), lambda: ring(step + 1, g, kind).start())
                     share(step, g, kind, 1).start()
 
-                on(owner(step, g, kind), take)
-        if step < far:
-            form(along(-way * step))
-        for kind in range(2):
-            for g in range(groups):
-                whose = owner(step, g, kind)
+                on(owner(step, kind), take)
+            if step == max(far - 1, 1) and g < groups - 1:
+                launch(g + 1, 0)
+                launch(g + 1, 1)
+            if step < far:
+                form(along(-way * step), g)
+            for kind in range(2):
+                whose = owner(step, kind)
                 on(None if whose is None else 1 - whose, lambda: share(step, g, kind, -1).wait_recv())
-        form(along(way * step))
+            form(along(way * step), g)
 
     def product(value, place, g, half):
         at = slice(half * size, (half + 1) * size)
@@ -217,47 +225,89 @@
         base[place, :, :size] = -taken[:, :size]
         base[place, :, size:] = under - taken[:, size:]
 
-    for g in range(groups):
+    def send_carry(g):
+        @pl.when(outer)
+        def _():
+            pass_on(g).start()
+
+    def begin(g, at_first):
         for place in range(nx - 1):
             prepare(g, place)
-
-        @pl.when(first)
+        if at_first:
+            return
+        right = slice(size, wide)
+        start = maps[0, g, 0, :size, right].astype(jnp.float32) + maps[0, g, 1, :size, right].astype(jnp.float32)
+        through = jnp.concatenate([-start, base[0, :, right]], axis=0)
+        rows = size + part
+        for place in range(1, nx):
+            high, lower = split(through)
+            both = jnp.dot(jnp.concatenate([high, lower], axis=0), maps[place, g, 0, :size, right],
+                           preferred_element_type=jnp.float32)
+            cross = jnp.dot(high, maps[place, g, 1, :size, right], preferred_element_type=jnp.float32)
+            through = -(both[:rows] + (both[rows:] + cross))
+            if place < nx - 1:
+                through = jnp.concatenate([through[:size], through[size:] + base[place, :, right]], axis=0)
+        skip[g] = through
+
+    def chain(g, at_first):
+        if g > 0:
+            begin(g, at_first)
+
+        @pl.when(outer)
         def _():
-            carry[g] = state[g, 0]
-
-        @pl.when(inner)
-        def _():
-            pass_carry = pass_on(g)
-            pass_carry.wait_recv()
-
-        top = carry[g]
+            low(g).wait_recv()
+
+        prepare(g, nx - 1)
+        if at_first:
+            top = state[g, 0]
+        else:
+            pass_on(g).wait_recv()
+            top = carry[g]
+            passed[g] = product3(top, skip[g, :size]) + (skip[g, size:] + base[nx - 1, :, size:])
+            send_carry(g)
         for place in range(nx):
-            if place == nx - 1:
-                @pl.when(outer)
-                def _():
-                    low(g).wait_recv()
-
-                prepare(g, place)
             result = base[place] - product(top, place, g, 0)
             done = top + result[:, :size]
             top = result[:, size:]
             if g < groups - 1:
                 state[g + 1, place] = done
-                if place == 0:
-                    @pl.when(inner)
-                    def _():
-                        low(g + 1).start()
+                if place == 0 and not at_first:
+                    low(g + 1).start()
             else:
                 ready[place] = done
 
                 @pl.when(x != place)
                 def _():
                     deliver(place, place).start()
-        passed[g] = top
-
-        @pl.when(outer)
+        if at_first:
+            passed[g] = top
+            send_carry(g)
+
+    def chain_where(condition, g, at_first):
+        @pl.when(condition)
         def _():
-            pass_on(g).start()
+            chain(g, at_first)
+
+    early = inner & (y <= 2)
+    spread(0)
+
+    @pl.when(first)
+    def _():
+        begin(0, True)
+        chain(0, True)
+
+    @pl.when(inner)
+    def _():
+        begin(0, False)
+
+    spread(1)
+    chain_where(first, 1, True)
+    chain_where(early, 0, False)
+    spread(2)
+    chain_where(y > 2, 0, False)
+    chain_where(inner, 1, False)
+    chain_where(first, 2, True)
+    chain_where(inner, 2, False)
 
     final[cols_of(x)] = ready[x]
     for k in range(1, nx):
@@ -274,7 +324,7 @@
                     ring(step, g, kind).wait_send()
                     share(step, g, kind, 1).wait_send()
 
-                on(owner(step, g, kind), finish)
+                on(owner(step, kind), finish)
     for place in range(nx):
         @pl.when(x != place)
         def _():
@@ -308,6 +358,7 @@
             vmem((cols, size), f32),
             vmem((groups, nx + 1, part, size), f32),
             vmem((nx, part, wide), f32),
+            vmem((groups, size + part, size), f32),
             vmem((groups, part, size), f32),
             vmem((groups, part, size), f32),
             vmem((nx, part, size), f32),

time: 105 us -> 107 us (1.019)
  Pallas kernels: 103 us -> 105 us
    pallas_call x1, Pallas kernels: 103 us -> 105 us  [local(): pl.pallas_call(functools.partial(kernel, n_rows, n_vecs, nx), out_shape=j...]
where the time goes in v3:
time: 107 us; the launch traced here: 106 us
  Pallas kernels  105 us (98%)
  local copies, waits for them, and re-layouts  1.57 us (1%)
    pallas_call x1, Pallas kernels, local(): pl.pallas_call(functools.partial(kernel, n_rows, n_vecs, nx), out_shape=j...  105 us

profile of v3, /device:TPU:126, one launch (start us, length us, event | category | flops | bytes accessed | tf_op | source)
XLA Modules:
  0.0 106.4 jit_solution(12549808666890602452)
XLA Ops:
  0.0 104.9 %rows.1 = f32[128,128]{1,0:T(8,128)} custom-call(f32[128,128]{1,0:T(8,128)} %x_ref.1, f32[3,1,8,256]{3,2,1,0:T(8,128)} %refl_ref.1), custom_call_target="tpu_custom_call" | custom-call | tf_op jit(solution)/shard_map/rows/pallas_call | solution.py:349
  104.9 1.6 %copy.3 = f32[128,128]{1,0:T(8,128)} copy(f32[128,128]{0,1:T(8,128)} %bitcast.1) | data formatting | bytes 131072 | tf_op jit(solution)/shard_map/transpose | solution.py:373

commit v4 on v3

--- a/solution.py
+++ b/solution.py
@@ -175,19 +175,18 @@
     def masked(place, g):
         return jnp.where((y * nx + place < n_rows - 1) | (lane < size), blocks[place, g], 0.0)
 
-    for g, inverse in enumerate(inverse_factors([masked(x, g) for g in range(groups)])):
-        factors[x, g] = inverse
-        if g == 0:
-            launch(0, 1)
+    def factor(*own):
+        for g, inverse in zip(own, inverse_factors([masked(x, g) for g in own])):
+            factors[x, g] = inverse
 
     def form(place, g):
         block = masked(place, g)
         full = product3(block.T, product3(factors[place, g], block))
         maps[place, g, 0], maps[place, g, 1] = split(full)
 
-    def spread(g):
-        form(x, g)
-        for step in range(1, far + 1):
+    def spread(slot):
+        here = [(slot - g, g) for g in range(groups) if 1 <= slot - g <= far]
+        for step, g in here:
             for kind in range(2):
                 def take():
                     ring_arrival(step, g, kind).wait_recv()
@@ -196,15 +195,23 @@
                     share(step, g, kind, 1).start()
 
                 on(owner(step, kind), take)
-            if step == max(far - 1, 1) and g < groups - 1:
-                launch(g + 1, 0)
-                launch(g + 1, 1)
+        if slot < groups:
+            launch(slot, 0)
+            if slot == 1:
+                factor(*range(1, groups))
+            launch(slot, 1)
+            form(x, slot)
+        for step, g in here:
             if step < far:
                 form(along(-way * step), g)
             for kind in range(2):
                 whose = owner(step, kind)
                 on(None if whose is None else 1 - whose, lambda: share(step, g, kind, -1).wait_recv())
             form(along(way * step), g)
+
+    factor(0)
+    launch(0, 1)
+    form(x, 0)
 
     def product(value, place, g, half):
         at = slice(half * size, (half + 1) * size)
@@ -250,9 +257,6 @@
         skip[g] = through
 
     def chain(g, at_first):
-        if g > 0:
-            begin(g, at_first)
-
         @pl.when(outer)
         def _():
             low(g).wait_recv()
@@ -283,31 +287,45 @@
             passed[g] = top
             send_carry(g)
 
-    def chain_where(condition, g, at_first):
+    early = inner & (y <= 2)
+    for slot in range(1, far + 1):
+        spread(slot)
+
+    @pl.when(first)
+    def _():
+        begin(0, True)
+        chain(0, True)
+
+    @pl.when(inner)
+    def _():
+        begin(0, False)
+
+    spread(far + 1)
+
+    @pl.when(first)
+    def _():
+        begin(1, True)
+
+    @pl.when(early)
+    def _():
+        chain(0, False)
+        begin(1, False)
+
+    for slot in range(far + 2, far + groups):
+        spread(slot)
+
+    @pl.when(y > 2)
+    def _():
+        chain(0, False)
+        begin(1, False)
+
+    for at_first, condition in ((True, first), (False, inner)):
         @pl.when(condition)
         def _():
-            chain(g, at_first)
-
-    early = inner & (y <= 2)
-    spread(0)
-
-    @pl.when(first)
-    def _():
-        begin(0, True)
-        chain(0, True)
-
-    @pl.when(inner)
-    def _():
-        begin(0, False)
-
-    spread(1)
-    chain_where(first, 1, True)
-    chain_where(early, 0, False)
-    spread(2)
-    chain_where(y > 2, 0, False)
-    chain_where(inner, 1, False)
-    chain_where(first, 2, True)
-    chain_where(inner, 2, False)
+            for g in range(1, groups):
+                if g > 1:
+                    begin(g, at_first)
+                chain(g, at_first)
 
     final[cols_of(x)] = ready[x]
     for k in range(1, nx):

time: 107 us -> 95.5 us (0.89)
  the two profiles are of different devices: /device:TPU:126 before, /device:TPU:116 now
where the time goes in v4:
time: 95.5 us; the launch traced here: 95.2 us
  Pallas kernels  93.7 us (98%)
  local copies, waits for them, and re-layouts  1.57 us (2%)
    pallas_call x1, Pallas kernels, local(): pl.pallas_call(functools.partial(kernel, n_rows, n_vecs, nx), out_shape=j...  93.7 us

profile of v4, /device:TPU:116, one launch (start us, length us, event | category | flops | bytes accessed | tf_op | source)
XLA Modules:
  0.0 95.2 jit_solution(16446971599093984185)
XLA Ops:
  0.0 93.7 %rows.1 = f32[128,128]{1,0:T(8,128)} custom-call(f32[128,128]{1,0:T(8,128)} %x_ref.1, f32[3,1,8,256]{3,2,1,0:T(8,128)} %refl_ref.1), custom_call_target="tpu_custom_call" | custom-call | tf_op jit(solution)/shard_map/rows/pallas_call | solution.py:367
  93.7 1.6 %copy.3 = f32[128,128]{1,0:T(8,128)} copy(f32[128,128]{0,1:T(8,128)} %bitcast.1) | data formatting | bytes 131072 | tf_op jit(solution)/shard_map/transpose | solution.py:391

commit v5 on v4

--- a/solution.py
+++ b/solution.py
@@ -52,8 +52,8 @@
         if size == 1:
             results = [result - corner for result, corner in zip(results, corners)]
         else:
-            halfway = [hdot(result, corner) for result, corner in zip(results, corners)]
-            results = [result - hdot(half, result) for result, half in zip(results, halfway)]
+            halfway = [product3(result, corner) for result, corner in zip(results, corners)]
+            results = [result - product3(half, result) for result, half in zip(results, halfway)]
         size = wide
     return [result / half for result, half in zip(results, halves)]
 
@@ -100,9 +100,15 @@
         return pl.ds(pl.multiple_of(place * part, part), part)
 
     sends = []
-    for k, peer in enumerate(chips + [partner]):
-        sends.append(remote(refl_ref.at[:, 0], blocks.at[x, :, rows_of(v)], ag_send.at[k], ag_recv.at[v], (r, peer)))
-        sends[-1].start()
+    halves = (slice(0, 1), slice(1, groups))
+
+    def shard(half, vec):
+        return blocks.at[x, halves[half], rows_of(vec)]
+
+    for half in range(2):
+        for k, peer in enumerate(chips + [partner]):
+            sends.append(remote(refl_ref.at[halves[half], 0], shard(half, v), ag_send.at[half, k], ag_recv.at[half, v], (r, peer)))
+            sends[-1].start()
 
     turned[...] = x_ref[...].T
     for k, peer in enumerate(peers):
@@ -116,19 +122,23 @@
         for g in range(groups):
             state[g, nx] = jnp.zeros((part, size), jnp.float32)
 
-    def arrived(vec):
-        remote(refl_ref.at[:, 0], blocks.at[x, :, rows_of(vec)], ag_send.at[0], ag_recv.at[vec], mate).wait_recv()
+    def arrived(half, vec):
+        remote(refl_ref.at[halves[half], 0], shard(half, vec), ag_send.at[half, 0], ag_recv.at[half, vec], mate).wait_recv()
 
     order = sorted(range(1, n_chips), key=lambda k: min(k, n_chips - k))
-    for k in order:
-        source = lax.rem(v - 2 * k + n_vecs, n_vecs)
-        arrived(source)
-        there = blocks.at[x, :, rows_of(source)]
-        sends.append(remote(there, there, ag_send.at[n_chips + k - 1], ag_recv.at[source], mate))
-        sends[-1].start()
-    arrived(partner)
-    for k in order:
-        arrived(lax.rem(partner - 2 * k + n_vecs, n_vecs))
+
+    def gather(half):
+        for k in order:
+            source = lax.rem(v - 2 * k + n_vecs, n_vecs)
+            arrived(half, source)
+            there = shard(half, source)
+            sends.append(remote(there, there, ag_send.at[half, n_chips + k - 1], ag_recv.at[half, source], mate))
+            sends[-1].start()
+        arrived(half, partner)
+        for k in order:
+            arrived(half, lax.rem(partner - 2 * k + n_vecs, n_vecs))
+
+    gather(0)
 
     far = nx // 2
     stores = (blocks, factors)
@@ -159,16 +169,8 @@
 
     launch(0, 0)
 
-    for k in range(1, nx):
-        source = along(-k)
-        remote(turned.at[cols_of(x)], state.at[0, source], in_send.at[0], in_recv.at[source], onward).wait_recv()
-
     def low(g):
         return remote(state.at[g, 0], state.at[g, nx], low_send.at[g], low_recv.at[g], above)
-
-    @pl.when(inner)
-    def _():
-        low(0).start()
 
     lane = lax.broadcasted_iota(jnp.int32, (size, wide), 1)
 
@@ -212,6 +214,7 @@
     factor(0)
     launch(0, 1)
     form(x, 0)
+    gather(1)
 
     def product(value, place, g, half):
         at = slice(half * size, (half + 1) * size)
@@ -288,7 +291,16 @@
             send_carry(g)
 
     early = inner & (y <= 2)
-    for slot in range(1, far + 1):
+    spread(1)
+    for k in range(1, nx):
+        source = along(-k)
+        remote(turned.at[cols_of(x)], state.at[0, source], in_send.at[0], in_recv.at[source], onward).wait_recv()
+
+    @pl.when(inner)
+    def _():
+        low(0).start()
+
+    for slot in range(2, far + 1):
         spread(slot)
 
     @pl.when(first)
@@ -305,6 +317,7 @@
     @pl.when(first)
     def _():
         begin(1, True)
+        chain(1, True)
 
     @pl.when(early)
     def _():
@@ -318,13 +331,16 @@
     def _():
         chain(0, False)
         begin(1, False)
+
+    @pl.when(inner)
+    def _():
+        chain(1, False)
 
     for at_first, condition in ((True, first), (False, inner)):
         @pl.when(condition)
         def _():
-            for g in range(1, groups):
-                if g > 1:
-                    begin(g, at_first)
+            for g in range(2, groups):
+                begin(g, at_first)
                 chain(g, at_first)
 
     final[cols_of(x)] = ready[x]
@@ -381,7 +397,7 @@
             vmem((groups, part, size), f32),
             vmem((nx, part, size), f32),
             vmem((cols, size), f32),
-            dma((n_vecs,)), dma((n_vecs,)), dma((nx,)), dma((nx,)),
+            dma((2, n_vecs)), dma((2, n_vecs)), dma((nx,)), dma((nx,)),
             dma((far, groups, 2)), dma((far, groups, 2)), dma((far, groups, 2)), dma((far, groups, 2)),
             dma((groups,)), dma((groups,)), dma((groups,)), dma((groups,)), dma((nx,)), dma((nx,)),
         ],

time: 95.5 us -> 93.3 us (0.977)
  the two profiles are of different devices: /device:TPU:116 before, /device:TPU:114 now
where the time goes in v5:
time: 93.3 us; the launch traced here: 93.1 us
  Pallas kernels  91.5 us (98%)
  local copies, waits for them, and re-layouts  1.57 us (2%)
    pallas_call x1, Pallas kernels, local(): pl.pallas_call(functools.partial(kernel, n_rows, n_vecs, nx), out_shape=j...  91.5 us

profile of v5, /device:TPU:114, one launch (start us, length us, event | category | flops | bytes accessed | tf_op | source)
XLA Modules:
  0.0 93.1 jit_solution(2228649261052084409)
XLA Ops:
  0.0 91.5 %rows.1 = f32[128,128]{1,0:T(8,128)} custom-call(f32[128,128]{1,0:T(8,128)} %x_ref.1, f32[3,1,8,256]{3,2,1,0:T(8,128)} %refl_ref.1), custom_call_target="tpu_custom_call" | custom-call | tf_op jit(solution)/shard_map/rows/pallas_call | solution.py:383
  91.6 1.6 %copy.3 = f32[128,128]{1,0:T(8,128)} copy(f32[128,128]{0,1:T(8,128)} %bitcast.1) | data formatting | bytes 131072 | tf_op jit(solution)/shard_map/transpose | solution.py:407

commit v6 on v5

--- a/solution.py
+++ b/solution.py
@@ -58,7 +58,7 @@
     return [result / half for result, half in zip(results, halves)]
 
 
-def kernel(n_rows, n_vecs, nx, x_ref, refl_ref, out_ref, blocks, factors, maps, turned, state, base, skip, carry,
+def kernel(n_rows, n_vecs, nx, x_ref, refl_ref, out_ref, blocks, factors, maps, turned, state, base, skip, alone, carry,
            passed, ready, final, ag_send, ag_recv, in_send, in_recv, ring_send, ring_recv, share_send,
            share_recv, low_send, low_recv, car_send, car_recv, fin_send, fin_recv):
     groups, size, wide = blocks.shape[1:]
@@ -155,17 +155,8 @@
         there = stores[kind].at[along(-sign * way * step), g]
         return remote(there, there, share_send.at[step - 1, g, kind], share_recv.at[step - 1, g, kind], mate)
 
-    def owner(step, kind):
-        return None if step < far else kind
-
-    def on(core_index, action):
-        if core_index is None:
-            action()
-        else:
-            pl.when(core == core_index)(action)
-
     def launch(g, kind):
-        on(owner(1, kind), lambda: ring(1, g, kind).start())
+        ring(1, g, kind).start()
 
     launch(0, 0)
 
@@ -190,13 +181,10 @@
         here = [(slot - g, g) for g in range(groups) if 1 <= slot - g <= far]
         for step, g in here:
             for kind in range(2):
-                def take():
-                    ring_arrival(step, g, kind).wait_recv()
-                    if step < far:
-                        on(owner(step + 1, kind), lambda: ring(step + 1, g, kind).start())
+                ring_arrival(step, g, kind).wait_recv()
+                if step < far:
+                    ring(step + 1, g, kind).start()
                     share(step, g, kind, 1).start()
-
-                on(owner(step, kind), take)
         if slot < groups:
             launch(slot, 0)
             if slot == 1:
@@ -204,12 +192,11 @@
             launch(slot, 1)
             form(x, slot)
         for step, g in here:
+            form(along(-way * step), g)
             if step < far:
-                form(along(-way * step), g)
-            for kind in range(2):
-                whose = owner(step, kind)
-                on(None if whose is None else 1 - whose, lambda: share(step, g, kind, -1).wait_recv())
-            form(along(way * step), g)
+                for kind in range(2):
+                    share(step, g, kind, -1).wait_recv()
+                form(along(way * step), g)
 
     factor(0)
     launch(0, 1)
@@ -257,7 +244,8 @@
             through = -(both[:rows] + (both[rows:] + cross))
             if place < nx - 1:
                 through = jnp.concatenate([through[:size], through[size:] + base[place, :, right]], axis=0)
-        skip[g] = through
+        skip[g, 0], skip[g, 1] = split(through[:size])
+        alone[g] = through[size:]
 
     def chain(g, at_first):
         @pl.when(outer)
@@ -270,7 +258,10 @@
         else:
             pass_on(g).wait_recv()
             top = carry[g]
-            passed[g] = product3(top, skip[g, :size]) + (skip[g, size:] + base[nx - 1, :, size:])
+            high, lower = split(top)
+            both = jnp.dot(jnp.concatenate([high, lower], axis=0), skip[g, 0], preferred_element_type=jnp.float32)
+            cross = jnp.dot(high, skip[g, 1], preferred_element_type=jnp.float32)
+            passed[g] = both[:part] + (both[part:] + cross) + (alone[g] + base[nx - 1, :, size:])
             send_carry(g)
         for place in range(nx):
             result = base[place] - product(top, place, g, 0)
@@ -290,7 +281,6 @@
             passed[g] = top
             send_carry(g)
 
-    early = inner & (y <= 2)
     spread(1)
     for k in range(1, nx):
         source = along(-k)
@@ -312,6 +302,10 @@
     def _():
         begin(0, False)
 
+    @pl.when(y == 1)
+    def _():
+        chain(0, False)
+
     spread(far + 1)
 
     @pl.when(first)
@@ -319,9 +313,12 @@
         begin(1, True)
         chain(1, True)
 
-    @pl.when(early)
+    @pl.when(y == 2)
     def _():
         chain(0, False)
+
+    @pl.when(inner & (y <= 2))
+    def _():
         begin(1, False)
 
     for slot in range(far + 2, far + groups):
@@ -354,11 +351,9 @@
     for step in range(1, far + 1):
         for kind in range(2):
             for g in range(groups):
-                def finish():
-                    ring(step, g, kind).wait_send()
+                ring(step, g, kind).wait_send()
+                if step < far:
                     share(step, g, kind, 1).wait_send()
-
-                on(owner(step, kind), finish)
     for place in range(nx):
         @pl.when(x != place)
         def _():
@@ -392,7 +387,8 @@
             vmem((cols, size), f32),
             vmem((groups, nx + 1, part, size), f32),
             vmem((nx, part, wide), f32),
-            vmem((groups, size + part, size), f32),
+            vmem((groups, 2, size, size), jnp.bfloat16),
+            vmem((groups, part, size), f32),
             vmem((groups, part, size), f32),
             vmem((groups, part, size), f32),
             vmem((nx, part, size), f32),

time: 93.3 us -> 93.9 us (level)
  no operation moved by 1% of the time
where the time goes in v6:
time: 93.9 us; the launch traced here: 93.7 us
  Pallas kernels  92.1 us (98%)
  local copies, waits for them, and re-layouts  1.57 us (2%)
    pallas_call x1, Pallas kernels, local(): pl.pallas_call(functools.partial(kernel, n_rows, n_vecs, nx), out_shape=j...  92.1 us

profile of v6, /device:TPU:114, one launch (start us, length us, event | category | flops | bytes accessed | tf_op | source)
XLA Modules:
  0.0 93.7 jit_solution(3197006944256291352)
XLA Ops:
  0.0 92.1 %rows.1 = f32[128,128]{1,0:T(8,128)} custom-call(f32[128,128]{1,0:T(8,128)} %x_ref.1, f32[3,1,8,256]{3,2,1,0:T(8,128)} %refl_ref.1), custom_call_target="tpu_custom_call" | custom-call | tf_op jit(solution)/shard_map/rows/pallas_call | solution.py:378
  92.1 1.6 %copy.3 = f32[128,128]{1,0:T(8,128)} copy(f32[128,128]{0,1:T(8,128)} %bitcast.1) | data formatting | bytes 131072 | tf_op jit(solution)/shard_map/transpose | solution.py:403

commit v7 on v5

--- a/solution.py
+++ b/solution.py
@@ -58,7 +58,7 @@
     return [result / half for result, half in zip(results, halves)]
 
 
-def kernel(n_rows, n_vecs, nx, x_ref, refl_ref, out_ref, blocks, factors, maps, turned, state, base, skip, carry,
+def kernel(n_rows, n_vecs, nx, x_ref, refl_ref, out_ref, blocks, factors, maps, turned, state, base, skip, alone, carry,
            passed, ready, final, ag_send, ag_recv, in_send, in_recv, ring_send, ring_recv, share_send,
            share_recv, low_send, low_recv, car_send, car_recv, fin_send, fin_recv):
     groups, size, wide = blocks.shape[1:]
@@ -257,7 +257,8 @@
             through = -(both[:rows] + (both[rows:] + cross))
             if place < nx - 1:
                 through = jnp.concatenate([through[:size], through[size:] + base[place, :, right]], axis=0)
-        skip[g] = through
+        skip[g, 0], skip[g, 1] = split(through[:size])
+        alone[g] = through[size:]
 
     def chain(g, at_first):
         @pl.when(outer)
@@ -270,7 +271,10 @@
         else:
             pass_on(g).wait_recv()
             top = carry[g]
-            passed[g] = product3(top, skip[g, :size]) + (skip[g, size:] + base[nx - 1, :, size:])
+            high, lower = split(top)
+            both = jnp.dot(jnp.concatenate([high, lower], axis=0), skip[g, 0], preferred_element_type=jnp.float32)
+            cross = jnp.dot(high, skip[g, 1], preferred_element_type=jnp.float32)
+            passed[g] = both[:part] + (both[part:] + cross) + (alone[g] + base[nx - 1, :, size:])
             send_carry(g)
         for place in range(nx):
             result = base[place] - product(top, place, g, 0)
@@ -290,7 +294,6 @@
             passed[g] = top
             send_carry(g)
 
-    early = inner & (y <= 2)
     spread(1)
     for k in range(1, nx):
         source = along(-k)
@@ -312,6 +315,10 @@
     def _():
         begin(0, False)
 
+    @pl.when(y == 1)
+    def _():
+        chain(0, False)
+
     spread(far + 1)
 
     @pl.when(first)
@@ -319,9 +326,12 @@
         begin(1, True)
         chain(1, True)
 
-    @pl.when(early)
+    @pl.when(y == 2)
     def _():
         chain(0, False)
+
+    @pl.when(inner & (y <= 2))
+    def _():
         begin(1, False)
 
     for slot in range(far + 2, far + groups):
@@ -392,7 +402,8 @@
             vmem((cols, size), f32),
             vmem((groups, nx + 1, part, size), f32),
             vmem((nx, part, wide), f32),
-            vmem((groups, size + part, size), f32),
+            vmem((groups, 2, size, size), jnp.bfloat16),
+            vmem((groups, part, size), f32),
             vmem((groups, part, size), f32),
             vmem((groups, part, size), f32),
             vmem((nx, part, size), f32),

time: 93.3 us -> 93.2 us (level)
  no operation moved by 1% of the time
where the time goes in v7:
time: 93.2 us; the launch traced here: 93 us
  Pallas kernels  91.4 us (98%)
  local copies, waits for them, and re-layouts  1.57 us (2%)
    pallas_call x1, Pallas kernels, local(): pl.pallas_call(functools.partial(kernel, n_rows, n_vecs, nx), out_shape=j...  91.4 us

profile of v7, /device:TPU:114, one launch (start us, length us, event | category | flops | bytes accessed | tf_op | source)
XLA Modules:
  0.0 93.0 jit_solution(3182621141574617965)
XLA Ops:
  0.0 91.4 %rows.1 = f32[128,128]{1,0:T(8,128)} custom-call(f32[128,128]{1,0:T(8,128)} %x_ref.1, f32[3,1,8,256]{3,2,1,0:T(8,128)} %refl_ref.1), custom_call_target="tpu_custom_call" | custom-call | tf_op jit(solution)/shard_map/rows/pallas_call | solution.py:393
  91.4 1.6 %copy.3 = f32[128,128]{1,0:T(8,128)} copy(f32[128,128]{0,1:T(8,128)} %bitcast.1) | data formatting | bytes 131072 | tf_op jit(solution)/shard_map/transpose | solution.py:418
